TPU v7x, 512 devices: a whole 4x4x16 slice. The times are simulated.
512 devices in a mesh: rows: 64 (over y, z), sub: 8 (over x, core).
Axes of the slice: x: 4, y: 4, z: 16, core: 2. Of those that a mesh axis runs over, the one named last changes fastest.
Arguments:
- affinity: bfloat16 [4096, 3, 256, 256], P(('rows', 'sub')), may hold values from 0.0099487305 to 1
- old_basis: bfloat16 [1048576, 64], P(('rows', 'sub')), may hold values from -1500 to 1500, as said below
- degrees: int32 [1048576], P(('rows', 'sub')), may hold values from 10 to 90
- column_blocks: int32 [4096, 3], P(('rows', 'sub')), may hold values from 0 to 4095, as said below
- reorder: int32 [4096, 256], P(('rows', 'sub')), may hold values from 0 to 255, each once within a row
Outputs:
- targets: float32 [1048576, 64], P(('rows', 'sub'))
Inputs may be any that keep to these rules, and one draw needn't show every extreme that they name: column_blocks[b, 0] = b; the other entries of row b are distinct, differ from b and lie within 2 of b; block row 0 names block 2. `old_basis`: entries of magnitude up to 1500.
All inputs are finite; a program needn't handle non-finite values.
Results may differ from a plain program's by a relative error of at most 0.0035.
Values may be sent and summed in bfloat16 or wider, within the bound.
A program may use at most 64 MiB of HBM per device.

v0:
```python
import math

import jax
import jax.numpy as jnp
from jax import lax
from jax.sharding import PartitionSpec as P

REACH = 2


def with_halo(cells, sides, width):
    for axis, dim in sides:
        count = lax.axis_size(axis)
        ends = count - 1
        head = lax.slice_in_dim(cells, 0, width, axis=dim)
        tail = lax.slice_in_dim(cells, cells.shape[dim] - width, cells.shape[dim], axis=dim)
        cells = jnp.concatenate(
            [
                lax.ppermute(tail, axis, [(i, (i + 1) % count) for i in range(ends)]),
                cells,
                lax.ppermute(head, axis, [((i + 1) % count, i) for i in range(ends)]),
            ],
            axis=dim,
        )
    return cells


def body(affinity, old_basis, degrees, column_blocks, reorder):
    count = affinity.shape[0]
    block = affinity.shape[-1]
    rows_here = old_basis.shape[0]
    width = REACH * block
    inverse_root = lax.rsqrt(degrees.astype(jnp.float32))[:, None]
    scaled = (inverse_root * old_basis.astype(jnp.float32)).astype(jnp.bfloat16)
    extended = with_halo(scaled, ((("rows", "sub"), 0),), width)
    ext_blocks = extended.reshape(count + 2 * REACH, block, -1)
    first_local = lax.axis_index(("rows", "sub")) * count - REACH
    fetched = ext_blocks[column_blocks - first_local]
    product = jnp.einsum("bkij,bkjr->bir", affinity, fetched, preferred_element_type=jnp.float32)
    image_rows = product.reshape(rows_here, -1) * inverse_root
    gram_local = jnp.einsum(
        "ir,is->rs",
        image_rows,
        image_rows,
        precision=lax.Precision.HIGHEST,
        preferred_element_type=jnp.float32,
    )
    gram_whole = lax.psum(gram_local, ("rows", "sub"))
    lower_factor = jnp.linalg.cholesky(gram_whole)
    solved = lax.linalg.triangular_solve(lower_factor, image_rows.T, left_side=True, lower=True)
    total_items = rows_here * lax.axis_size("rows") * lax.axis_size("sub")
    clustered = (solved.T * math.sqrt(total_items)).reshape(count, block, -1)
    targets = jnp.take_along_axis(clustered, reorder[:, :, None], axis=1)
    return targets.reshape(rows_here, -1)


def solution(mesh):
    placed = (
        P(("rows", "sub"), None, None, None),
        P(("rows", "sub"), None),
        P(("rows", "sub")),
        P(("rows", "sub"), None),
        P(("rows", "sub"), None),
    )
    return jax.shard_map(
        body, mesh=mesh, in_specs=placed, out_specs=P(("rows", "sub"), None), check_vma=False
    )
```

profile of v0, /device:TPU:1, one launch (start us, length us, event | category | flops | bytes accessed | tf_op | source)
XLA Modules:
  0.0 184.1 jit_solution(14028861206709264188)
XLA Ops:
  0.0 0.0 copy-start
  0.0 0.9 convert_rsqrt_fusion
  0.9 1.1 multiply_convert_fusion
  2.0 0.7 fusion.6
  2.6 4.5 %collective-permute-start = (bf16[512,64]{0,1:T(8,128)(2,1)}, bf16[512,64]{0,1:T(8,128)(2,1)S(1)}, u32[]{:S(2)}, u32[]{:S(2)}) collective-permute-start(bf16[512,64]{0,1:T(8,128)(2,1)} %get-tuple-element.5), channel_id=1, source_target_pairs={{0,1},{1,2},{2,3},{3,4},{4,5},{5,6},{6,7},{7,8},{8,9},{9,10},{10,1... | collective-permute-start | bytes 196616 | tf_op jit(solution)/shard_map/ppermute | solution.py:19
  7.1 5.5 %collective-permute-start.1 = (bf16[512,64]{0,1:T(8,128)(2,1)}, bf16[512,64]{0,1:T(8,128)(2,1)S(1)}, u32[]{:S(2)}, u32[]{:S(2)}) collective-permute-start(bf16[512,64]{0,1:T(8,128)(2,1)} %get-tuple-element.6), channel_id=1, source_target_pairs={{1,0},{2,1},{3,2},{4,3},{5,4},{6,5},{7,6},{8,7},{9,8},{10,9},{11,1... | collective-permute-start | bytes 196616 | tf_op jit(solution)/shard_map/ppermute | solution.py:21
  12.7 1.3 fusion.5
  14.0 1.3 compare_and_fusion
  15.2 0.7 compare_select_fusion.1
  15.9 0.1 copy.12
  16.0 0.6 reshape.48
  16.6 0.7 copy.25
  17.3 1.3 broadcast_in_dim.17
  18.6 1.2 pad_clamp_fusion
  19.8 0.0 collective-permute-done
  19.8 0.0 collective-permute-done.1
  19.8 1.6 gather_fusion
  21.5 0.0 copy-done
  21.5 2.2 %fusion = f32[8,64,256]{2,1,0:T(8,128)S(1)} fusion(bf16[8,3,256,64]{2,3,1,0:T(8,128)(2,1)} %bitcast.41, bf16[8,3,256,256]{3,2,1,0:T(8,128)(2,1)S(1)} %copy-done, f32[8,256]{1,0:T(8,128)S(1)} %mul.42), kind=kOutput, calls=%fused_computation.4 | convolution fusion | flops 201457664 | bytes 4464640 | tf_op jit(solution)/shard_map/bkij,bkjr->bir/dot_general | solution.py:39
  23.7 0.0 copy-start.1
  23.7 0.8 copy-done.1
  24.5 0.6 convolution_bitcast_fusion.1
  25.0 106.8 %psum.7 = f32[64,64]{0,1:T(8,128)S(1)} all-reduce(f32[64,64]{0,1:T(8,128)S(1)} %convolution_bitcast_fusion.1), channel_id=1, replica_groups=mesh['rows'=64,'sub'=8] {'rows','sub'}, use_global_device_ids=true, to_apply=%region_0.0 | all-reduce | flops 4096 | bytes 32768 | tf_op jit(solution)/shard_map/psum | solution.py:48
  131.9 0.1 copy.16
  132.0 5.8 %cholesky.16 = f32[64,64]{1,0:T(8,128)S(1)} custom-call(f32[64,64]{1,0:T(8,128)S(1)} %fusion.4), custom_call_target="Cholesky" | custom-call | tf_op jit(solution)/shard_map/jit(cholesky)/cholesky | solution.py:49
  137.8 0.7 compare_reduce_fusion
  138.6 0.7 fusion.2
  139.3 4.9 %custom-call.6 = f32[1,64,64]{1,2,0:T(8,128)S(1)} custom-call(f32[1,64,64]{2,1,0:T(8,128)S(1)} %fusion.2), custom_call_target="InvertDiagBlocksLowerTriangular" | custom-call | tf_op jit(solution)/shard_map/triangular_solve | solution.py:50
  144.2 1.1 copy.24
  145.3 1.4 convolution_multiply_fusion
  146.7 2.4 %copy.22 = f32[2048,64]{1,0:T(8,128)} copy(f32[2048,64]{0,1:T(8,128)} %convolution_multiply_fusion) | data formatting | bytes 1048576 | tf_op jit(solution)/shard_map/reshape | solution.py:52
  149.1 0.0 copy-start.2
  149.1 30.1 %gather_fusion.1 = f32[2048,64]{1,0:T(8,128)} fusion(f32[8,256,64]{2,1,0:T(8,128)} %bitcast.39, s32[2048]{0:T(1024)S(1)} %bitcast.38), kind=kCustom, calls=%fused_computation.1 | custom fusion | bytes 1064960 | tf_op jit(solution)/shard_map/jit(take_along_axis)/gather | solution.py:53
  179.2 0.0 copy-done.2
  179.2 2.6 %broadcast_select_fusion = f32[2048,64]{1,0:T(8,128)} fusion(f32[2048,64]{1,0:T(8,128)} %gather_fusion.1, pred[2048]{0:T(1024)(128)(4,1)S(1)} %copy-done.2), kind=kLoop, calls=%fused_computation.7 | loop fusion | flops 131072 | bytes 1050624 | tf_op jit(solution)/shard_map/jit(take_along_axis)/select_n | solution.py:53
  181.7 2.3 %copy.18 = f32[2048,64]{0,1:T(8,128)} copy(f32[2048,64]{1,0:T(8,128)} %broadcast_select_fusion) | data formatting | bytes 1048576 | tf_op jit(solution)/shard_map/jit(take_along_axis)/select_n | solution.py:53
  (5 shorter events, 0.1 us)
Async XLA Ops:
  0.0 21.5 %copy-start = (bf16[8,3,256,256]{3,2,1,0:T(8,128)(2,1)S(1)}, bf16[8,3,256,256]{3,2,1,0:T(8,128)(2,1)}, u32[]{:S(2)}) copy-start(bf16[8,3,256,256]{3,2,1,0:T(8,128)(2,1)} %param.5) | copy-start | bytes 9437188
  2.6 17.2 %collective-permute-start = (bf16[512,64]{0,1:T(8,128)(2,1)}, bf16[512,64]{0,1:T(8,128)(2,1)S(1)}, u32[]{:S(2)}, u32[]{:S(2)}) collective-permute-start(bf16[512,64]{0,1:T(8,128)(2,1)} %get-tuple-element.5), channel_id=1, source_target_pairs={{0,1},{1,2},{2,3},{3,4},{4,5},{5,6},{6,7},{7,8},{8,9},{9,10},{10,1... | collective-permute-start | bytes 196616 | tf_op jit(solution)/shard_map/ppermute | solution.py:19
  7.1 12.7 %collective-permute-start.1 = (bf16[512,64]{0,1:T(8,128)(2,1)}, bf16[512,64]{0,1:T(8,128)(2,1)S(1)}, u32[]{:S(2)}, u32[]{:S(2)}) collective-permute-start(bf16[512,64]{0,1:T(8,128)(2,1)} %get-tuple-element.6), channel_id=1, source_target_pairs={{1,0},{2,1},{3,2},{4,3},{5,4},{6,5},{7,6},{8,7},{9,8},{10,9},{11,1... | collective-permute-start | bytes 196616 | tf_op jit(solution)/shard_map/ppermute | solution.py:21
  23.7 0.8 copy-start.1
  149.1 30.1 %copy-start.2 = (pred[2048]{0:T(1024)(128)(4,1)S(1)}, pred[2048]{0:T(1024)(128)(4,1)}, u32[]{:S(2)}) copy-start(pred[2048]{0:T(1024)(128)(4,1)} %broadcast_in_dim.17) | copy-start | bytes 6148
where the time goes:
time: 185 us; the launch traced here: 184 us
  blocking collectives  107 us (58%)
  local copies, waits for them, and re-layouts  41.8 us (23%)
  other arithmetic  21.2 us (11%)
  starting transfers between devices  10 us (5%)
  matrix products  4.17 us (2%)
    psum x1, blocking collectives, body(): gram_whole = lax.psum(gram_local, ('rows', 'sub'))  107 us
    gather x1, local copies, waits for them, and re-layouts, body(): targets = jnp.take_along_axis(clustered, reorder[:, :, None], axis=1)  30.1 us
    another operation x3, other arithmetic, body(): lower_factor = jnp.linalg.cholesky(gram_whole)  6.6 us
    another operation x2, other arithmetic, body(): lax.linalg.triangular_solve(lower_factor, image_rows.T, left_side=True, l...  5.59 us
    ppermute x1, starting transfers between devices, with_halo(): lax.ppermute(head, axis, [((i + 1) % count, i) for i in range(ends)])  5.54 us
    ppermute x1, starting transfers between devices, with_halo(): lax.ppermute(tail, axis, [(i, (i + 1) % count) for i in range(ends)])  4.49 us
  transfers between devices with their start and end apart: 2, of which 0 were waited for; matrix products, arithmetic and copies ran while one was open for 4% of the time, Pallas kernels for 0%

commit v1 on v0

v1 whole, which is shorter than its diff:
```python
import functools
import math

import jax
import jax.numpy as jnp
from jax import lax
from jax.experimental import pallas as pl
from jax.experimental.pallas import tpu as pltpu
from jax.sharding import PartitionSpec as P

MESH = pl.DeviceIdType.MESH
REACH = 2
NT = (((1,), (1,)), ((), ()))
F32 = jnp.float32
BF16 = jnp.bfloat16


def dot(a, b):
    return jnp.dot(a, b, preferred_element_type=F32)


def dot_nt(a, b):
    return lax.dot_general(a, b, NT, preferred_element_type=F32)


def front_kernel(
    dims,
    cols_ref, aff_hbm, basis_hbm, deg_hbm, reorder_hbm,
    gram_out, perm_out,
    aff, basis, deg, reorder, own, ext, iroot, acc0, parts,
    gpack, rs_buf, z_src, z_buf, ag_src, ag_buf,
    in_sem, aff_sem, halo_send, halo_recv, rs_send, rs_recv, z_send, z_recv, ag_send, ag_recv, out_sem,
):
    nz, ny, ns, count, block = dims
    plane = ny * ns
    total = plane * nz
    row, sub = lax.axis_index("rows"), lax.axis_index("sub")
    y, z = row // nz, row % nz
    mine = y * ns + sub
    linear = row * ns + sub

    def plane_id(q):
        return ((q // ns) * nz + z, q % ns)

    def z_id(w):
        return (y * nz + w, sub)

    def line_id(i):
        return (i // ns, i % ns)

    right = line_id((linear + 1) % total)
    left = line_id((linear + total - 1) % total)

    barrier = pltpu.get_barrier_semaphore()

    def signal(device):
        pl.semaphore_signal(barrier, inc=1, device_id=device, device_id_type=MESH)

    signal(left)
    signal(right)

    @pl.loop(1, nz)
    def _(d):
        signal(z_id((z + d) % nz))

    @pl.loop(1, plane)
    def _(d):
        signal(plane_id((mine + d) % plane))

    basis_in = pltpu.make_async_copy(basis_hbm, basis, in_sem.at[0])
    deg_in = pltpu.make_async_copy(deg_hbm, deg, in_sem.at[1])
    reorder_in = pltpu.make_async_copy(reorder_hbm, reorder, in_sem.at[2])
    deg_in.start()
    basis_in.start()

    def aff_in(b):
        return pltpu.make_async_copy(aff_hbm.at[b], aff.at[b], aff_sem.at[b])

    inner = tuple(range(REACH, count - REACH))
    outer = tuple(range(REACH)) + tuple(range(count - REACH, count))
    for b in inner + outer:
        aff_in(b).start()
    reorder_in.start()

    deg_in.wait()
    root = lax.rsqrt(deg[...].astype(F32))
    for b in range(count):
        for h in range(block // 128):
            r = b * (block // 128) + h
            iroot[b, :, h * 128 : (h + 1) * 128] = root[r : r + 1, :]
    basis_in.wait()
    for b in range(count):
        s = (basis[:, b * block : (b + 1) * block].astype(F32) * iroot[b]).astype(BF16)
        own[b] = s
        ext[b + REACH] = s

    pl.semaphore_wait(barrier, 2 + (nz - 1) + (plane - 1))

    to_right = pltpu.make_async_remote_copy(
        own.at[pl.ds(count - REACH, REACH)], ext.at[pl.ds(0, REACH)],
        halo_send.at[0], halo_recv.at[0], device_id=right, device_id_type=MESH)
    to_left = pltpu.make_async_remote_copy(
        own.at[pl.ds(0, REACH)], ext.at[pl.ds(count + REACH, REACH)],
        halo_send.at[1], halo_recv.at[1], device_id=left, device_id_type=MESH)
    to_right.start()
    to_left.start()

    first = linear * count

    def finish(b, acc, gram):
        image = acc * iroot[b]
        hi = image.astype(BF16)
        rest = image - hi.astype(F32)
        mid = rest.astype(BF16)
        lo = (rest - mid.astype(F32)).astype(BF16)
        rank = hi.shape[0]
        parts[b, :rank, :] = hi
        parts[b, rank:, :] = mid
        g1 = dot_nt(jnp.concatenate([hi, mid, lo], axis=0), hi)
        g2 = dot_nt(jnp.concatenate([hi, mid], axis=0), mid)
        g3 = dot_nt(hi, lo)
        small = g1[2 * rank :] + g2[rank:] + g3
        cross = g1[rank : 2 * rank] + g2[:rank]
        return gram + (g1[:rank] + (cross + small))

    rank = basis.shape[0]

    def early(b, gram):
        aff_in(b).wait()
        acc = dot_nt(own[b], aff[b, 0])
        for k in range(1, 3):
            acc += dot_nt(own[jnp.clip(cols_ref[k, b] - first, 0, count - 1)], aff[b, k])
        return finish(b, acc, gram)

    gram = lax.fori_loop(REACH, count - REACH, early, jnp.zeros((rank, rank), F32))

    def outer_block(j):
        return j + (count - 2 * REACH) * (j // REACH)

    @pl.loop(0, 2 * REACH)
    def _(j):
        b = outer_block(j)
        aff_in(b).wait()
        acc0[j] = dot_nt(own[b], aff[b, 0])

    to_right.wait()
    to_left.wait()

    def late(j, gram):
        b = outer_block(j)
        acc = acc0[j]
        for k in range(1, 3):
            acc += dot_nt(ext[jnp.clip(cols_ref[k, b] - first + REACH, 0, count + 2 * REACH - 1)], aff[b, k])
        return finish(b, acc, gram)

    gram = lax.fori_loop(0, 2 * REACH, late, gram)

    half = rank // 2
    packed = jnp.concatenate([gram[:half], gram[half:]], axis=1)
    per = half // plane
    for q in range(plane):
        gpack[q] = packed[q * per : (q + 1) * per]

    def rs_copy(d):
        q = (mine + d) % plane
        return pltpu.make_async_remote_copy(
            gpack.at[q], rs_buf.at[d - 1], rs_send.at[d - 1], rs_recv.at[d - 1],
            device_id=plane_id(q), device_id_type=MESH)

    def z_copy(d):
        return pltpu.make_async_remote_copy(
            z_src, z_buf.at[d - 1], z_send.at[d - 1], z_recv.at[d - 1],
            device_id=z_id((z + d) % nz), device_id_type=MESH)

    def ag_copy(d):
        q = (mine + d) % plane
        return pltpu.make_async_remote_copy(
            ag_src, ag_buf.at[mine], ag_send.at[d - 1], ag_recv.at[d - 1],
            device_id=plane_id(q), device_id_type=MESH)

    @pl.loop(1, plane)
    def _(d):
        rs_copy(d).start()

    reorder_in.wait()
    ids = lax.broadcasted_iota(jnp.int32, (block, block), 0)

    @pl.loop(0, count)
    def _(b):
        pick = jnp.where(ids == reorder[pl.ds(b, 1), :], 1.0, 0.0).astype(BF16)
        parts[b] = dot(parts[b], pick).astype(BF16)

    perm_copy = pltpu.make_async_copy(parts, perm_out, out_sem)
    perm_copy.start()

    @pl.loop(1, plane)
    def _(d):
        rs_copy(d).wait_recv()

    z_src[...] = gpack[mine] + jnp.sum(rs_buf[...], axis=0)

    @pl.loop(1, nz)
    def _(d):
        z_copy(d).start()

    @pl.loop(1, plane)
    def _(d):
        rs_copy(d).wait_send()

    @pl.loop(1, nz)
    def _(d):
        z_copy(d).wait_recv()

    chunk = z_src[...] + jnp.sum(z_buf[...], axis=0)
    ag_src[...] = chunk
    ag_buf[mine] = chunk

    @pl.loop(1, plane)
    def _(d):
        ag_copy(d).start()

    @pl.loop(1, nz)
    def _(d):
        z_copy(d).wait_send()

    perm_copy.wait()

    @pl.loop(1, plane)
    def _(d):
        ag_copy(d).wait()

    for q in range(plane):
        gram_out[q * per : (q + 1) * per] = ag_buf[q]


def back_kernel(scale, gram_ref, perm_hbm, out_hbm, perm, out, in_sem, out_sem):
    count, depth, block = perm.shape
    rank = depth // 2
    half = rank // 2
    tiles = rank // 8

    def perm_in(b):
        return pltpu.make_async_copy(perm_hbm.at[b], perm.at[b], in_sem.at[b])

    for b in range(count):
        perm_in(b).start()

    packed = gram_ref[...]
    low = pltpu.roll(packed, rank, 1)
    lane = lax.broadcasted_iota(jnp.int32, (8, 2 * rank), 1)
    sublane = lax.broadcasted_iota(jnp.int32, (8, 2 * rank), 0)
    state = []
    for t in range(tiles):
        source = low if t < tiles // 2 else packed
        r = (8 * t) % half
        eye = jnp.where(lane == sublane + 8 * t, 1.0, 0.0)
        state.append(jnp.where(lane < rank, eye, source[r : r + 8]))

    def row(v, j):
        return jnp.broadcast_to(v[j : j + 1, :], v.shape)

    rows = []
    for t in range(tiles):
        cols = []
        for j in range(8):
            k = rank + 8 * t + j
            cols.append([jnp.broadcast_to(state[v][:, k : k + 1], (8, 2 * rank)) for v in range(t, tiles)])
        pivots = None
        mults = []
        pivot_rows = []
        for j in range(8):
            pivot = row(cols[j][0], j)
            pivots = pivot if pivots is None else jnp.where(sublane == j, pivot, pivots)
            inv = 1.0 / pivot
            mult = [c * inv for c in cols[j]]
            mult[0] = jnp.where(sublane > j, mult[0], 0.0)
            for jj in range(j + 1, 8):
                top = row(cols[jj][0], j)
                cols[jj] = [c - m * top for c, m in zip(cols[jj], mult)]
            pivot_row = row(state[t], j)
            state[t] = state[t] - mult[0] * pivot_row
            mults.append(mult)
            pivot_rows.append(pivot_row)
        for v in range(t + 1, tiles):
            upd = mults[0][v - t] * pivot_rows[0]
            for j in range(1, 8):
                upd = upd + mults[j][v - t] * pivot_rows[j]
            state[v] = state[v] - upd
        rows.append(state[t] * (lax.rsqrt(pivots) * scale))

    inverse = jnp.concatenate(rows, axis=0)[:, :rank]
    hi = inverse.astype(BF16)
    mid = (inverse - hi.astype(F32)).astype(BF16)
    left = jnp.concatenate(
        [jnp.concatenate([hi, hi], axis=1), jnp.concatenate([mid, mid], axis=1)], axis=0)

    def out_copy(b):
        cols = pl.ds(b * block, block)
        return pltpu.make_async_copy(out.at[:, cols], out_hbm.at[:, cols], out_sem.at[b])

    for b in range(count):
        perm_in(b).wait()
        both = dot(left, perm[b])
        out[:, b * block : (b + 1) * block] = both[:rank] + both[rank:]
        out_copy(b).start()
    for b in range(count):
        out_copy(b).wait()


def body(ny, nz, ns, affinity, old_basis, degrees, column_blocks, reorder):
    count, _, block, _ = affinity.shape
    rows_here, rank = old_basis.shape
    plane = ny * ns
    per = rank // 2 // plane
    anywhere = pl.BlockSpec(memory_space=pl.ANY)
    vmem = pl.BlockSpec(memory_space=pltpu.VMEM)
    dma = pltpu.SemaphoreType.DMA
    gram, perm = pl.pallas_call(
        functools.partial(front_kernel, (nz, ny, ns, count, block)),
        name="front",
        out_shape=(
            jax.ShapeDtypeStruct((rank // 2, 2 * rank), F32),
            jax.ShapeDtypeStruct((count, 2 * rank, block), BF16),
        ),
        in_specs=[pl.BlockSpec(memory_space=pltpu.SMEM)] + [anywhere] * 4,
        out_specs=(vmem, anywhere),
        scratch_shapes=[
            pltpu.VMEM(affinity.shape, BF16),
            pltpu.VMEM((rank, rows_here), BF16),
            pltpu.VMEM((rows_here // 128, 128), jnp.int32),
            pltpu.VMEM(reorder.shape, jnp.int32),
            pltpu.VMEM((count, rank, block), BF16),
            pltpu.VMEM((count + 2 * REACH, rank, block), BF16),
            pltpu.VMEM((count, 1, block), F32),
            pltpu.VMEM((2 * REACH, rank, block), F32),
            pltpu.VMEM((count, 2 * rank, block), BF16),
            pltpu.VMEM((plane, per, 2 * rank), F32),
            pltpu.VMEM((plane - 1, per, 2 * rank), F32),
            pltpu.VMEM((per, 2 * rank), F32),
            pltpu.VMEM((nz - 1, per, 2 * rank), F32),
            pltpu.VMEM((per, 2 * rank), F32),
            pltpu.VMEM((plane, per, 2 * rank), F32),
            dma((3,)),
            dma((count,)),
            dma((2,)),
            dma((2,)),
            dma((plane - 1,)),
            dma((plane - 1,)),
            dma((nz - 1,)),
            dma((nz - 1,)),
            dma((plane - 1,)),
            dma((plane - 1,)),
            dma,
        ],
        compiler_params=pltpu.CompilerParams(collective_id=0, has_side_effects=True),
    )(column_blocks.T, affinity, old_basis.T, degrees.reshape(-1, 128), reorder)
    items = rows_here * lax.axis_size("rows") * lax.axis_size("sub")
    out = pl.pallas_call(
        functools.partial(back_kernel, math.sqrt(items)),
        name="back",
        out_shape=jax.ShapeDtypeStruct((rank, rows_here), F32),
        in_specs=[vmem, anywhere],
        out_specs=anywhere,
        scratch_shapes=[
            pltpu.VMEM((count, 2 * rank, block), BF16),
            pltpu.VMEM((rank, rows_here), F32),
            dma((count,)),
            dma((count,)),
        ],
    )(gram, perm)
    return out.T


def solution(mesh):
    rows, ns = mesh.shape["rows"], mesh.shape["sub"]
    nz = 16 if rows % 16 == 0 else rows // 2
    both = P(("rows", "sub"))
    return jax.shard_map(
        functools.partial(body, rows // nz, nz, ns),
        mesh=mesh, in_specs=(both,) * 5, out_specs=both, check_vma=False,
    )
```

time: 185 us -> 48.1 us (0.26)
  blocking collectives: 107 us -> 0 us
  Pallas kernels: 0 us -> 47.8 us
  local copies, waits for them, and re-layouts: 41.8 us -> 0 us
  other arithmetic: 21.2 us -> 0 us
  starting transfers between devices: 10 us -> 0 us
  matrix products: 4.17 us -> 0 us
    psum x1 -> x0, blocking collectives: 107 us -> none  [body(): gram_whole = lax.psum(gram_local, ('rows', 'sub'))]
    pallas_call x0 -> x2, Pallas kernels: none -> 47.8 us  [the longest x1 42.7 us: body(): pl.pallas_call(functools.partial(front_kernel, (nz, ny, ns, count, block)...]
    gather x2 -> x0, local copies, waits for them, and re-layouts: 31.7 us -> none  [the longest x1 30.1 us: body(): targets = jnp.take_along_axis(clustered, reorder[:, :, None], axis=1)]
    another operation x5 -> x0, other arithmetic: 12.2 us -> none  [the longest x3 6.6 us: body(): lower_factor = jnp.linalg.cholesky(gram_whole)]
    ppermute x2 -> x0, starting transfers between devices: 10 us -> none  [the longest x1 5.54 us: with_halo(): lax.ppermute(head, axis, [((i + 1) % count, i) for i in range(ends)])]
    select_n x2 -> x0, other arithmetic: 3.24 us -> none  [the longest x1 2.55 us: body(): targets = jnp.take_along_axis(clustered, reorder[:, :, None], axis=1)]
    dot_general x2 -> x0, matrix products: 2.76 us -> none  [the longest x1 2.19 us: body(): jnp.einsum('bkij,bkjr->bir', affinity, fetched, preferred_element_type=jn...]
    reshape x2 -> x0, local copies, waits for them, and re-layouts: 2.44 us -> none  [the longest x1 2.41 us: body(): clustered = (solved.T * math.sqrt(total_items)).reshape(count, block, -1)]
  transfers between devices with their start and end apart: 2 -> 0, of which waited for: 0 -> 0; matrix products, arithmetic and copies ran while one was open for 4% -> 0% of each run, Pallas kernels for 0% -> 0%
where the time goes in v1:
time: 48.1 us; the launch traced here: 47.8 us
  Pallas kernels  47.8 us (99%)
    pallas_call x1, Pallas kernels, body(): pl.pallas_call(functools.partial(front_kernel, (nz, ny, ns, count, block)...  42.7 us
    pallas_call x1, Pallas kernels, body(): pl.pallas_call(functools.partial(back_kernel, math.sqrt(items)), name='ba...  5.15 us

profile of v1, /device:TPU:1, one launch (start us, length us, event | category | flops | bytes accessed | tf_op | source)
XLA Modules:
  0.0 47.8 jit_solution(301502056638394334)
XLA Ops:
  0.0 42.7 %front.1 = (f32[32,128]{1,0:T(8,128)}, bf16[8,128,256]{2,1,0:T(8,128)(2,1)}) custom-call(s32[3,8]{1,0:T(4,128)} %bitcast.6, bf16[8,3,256,256]{3,2,1,0:T(8,128)(2,1)} %aff_hbm.1, bf16[64,2048]{1,0:T(8,128)(2,1)} %bitcast.4, s32[16,128]{1,0:T(8,128)} %bitcast.5, s32[8,256]{1,0:T(8,128)} %reorder_hbm.1), custom_call_target="tpu_custom_call" | custom-call | tf_op jit(solution)/shard_map/front/pallas_call | solution.py:318
  42.7 5.1 %back.1 = f32[64,2048]{1,0:T(8,128)} custom-call(f32[32,128]{1,0:T(8,128)} %get-tuple-element.7.gram_ref, bf16[8,128,256]{2,1,0:T(8,128)(2,1)} %get-tuple-element.8.perm_hbm), custom_call_target="tpu_custom_call" | custom-call | tf_op jit(solution)/shard_map/back/pallas_call | solution.py:358

commit v2 on v1

v2 whole, which is shorter than its diff:
```python
import functools
import math

import jax
import jax.numpy as jnp
from jax import lax
from jax.experimental import pallas as pl
from jax.experimental.pallas import tpu as pltpu
from jax.sharding import PartitionSpec as P

MESH = pl.DeviceIdType.MESH
REACH = 2
NT = (((1,), (1,)), ((), ()))
F32 = jnp.float32
BF16 = jnp.bfloat16


def dot(a, b):
    return jnp.dot(a, b, preferred_element_type=F32)


def dot_nt(a, b):
    return lax.dot_general(a, b, NT, preferred_element_type=F32)


def wrap(value, size):
    return jnp.where(value >= size, value - size, value)


def around(offset, size):
    return min(offset, size - offset)


def front_kernel(
    dims,
    cols_hbm, aff_hbm, basis_hbm, deg_hbm, reorder_hbm,
    gram_out, perm_out,
    cols, aff, basis, deg, reorder, halo, halo_deg, ext, iroot, parts,
    gpack, rs_buf, z_src, z_buf, ag_src, ag_buf,
    in_sem, aff_sem, halo_send, halo_recv, rs_send, rs_recv, z_send, z_recv, ag_send, ag_recv,
):
    nz, ny, ns, count, block = dims
    plane = ny * ns
    total = plane * nz
    rank = basis.shape[0]
    row, sub = lax.axis_index("rows"), lax.axis_index("sub")
    y, z = row // nz, row % nz
    mine = y * ns + sub
    linear = row * ns + sub

    up, down = wrap(linear + 1, total), wrap(linear + total - 1, total)
    right = (up // ns, up % ns)
    left = (down // ns, down % ns)
    ys = [wrap(y + d, ny) for d in range(ny)]
    subs = [wrap(sub + d, ns) for d in range(ns)]
    plane_offsets = sorted(
        ((dy, ds) for dy in range(ny) for ds in range(ns) if dy or ds),
        key=lambda o: -(2 * around(o[0], ny) + around(o[1], ns)))
    plane_ids = [(ys[dy] * nz + z, subs[ds]) for dy, ds in plane_offsets]
    plane_slots = [ys[dy] * ns + subs[ds] for dy, ds in plane_offsets]
    z_offsets = sorted(range(1, nz), key=lambda d: -around(d, nz))
    z_ids = [(y * nz + wrap(z + d, nz), sub) for d in z_offsets]

    barrier = pltpu.get_barrier_semaphore()

    def signal(device):
        pl.semaphore_signal(barrier, inc=1, device_id=device, device_id_type=MESH)

    def remote(src, dst, send, recv, device):
        return pltpu.make_async_remote_copy(
            src, dst, send, recv, device_id=device, device_id_type=MESH)

    def drain(ref, sem):
        pltpu.make_async_copy(ref, ref, sem).wait()

    signal(left)
    signal(right)

    deg_in = pltpu.make_async_copy(deg_hbm, deg, in_sem.at[0])
    basis_in = pltpu.make_async_copy(basis_hbm, basis, in_sem.at[1])
    cols_in = pltpu.make_async_copy(cols_hbm, cols, in_sem.at[2])
    reorder_in = pltpu.make_async_copy(reorder_hbm, reorder, in_sem.at[3])

    def aff_in(b):
        return pltpu.make_async_copy(aff_hbm.at[b], aff.at[b], aff_sem.at[b])

    inner = tuple(range(REACH, count - REACH))
    outer = tuple(range(REACH)) + tuple(range(count - REACH, count))
    deg_in.start()
    basis_in.start()
    cols_in.start()
    for b in inner:
        aff_in(b).start()
    for device in plane_ids + z_ids:
        signal(device)
    for b in outer:
        aff_in(b).start()
    reorder_in.start()

    pl.semaphore_wait(barrier, 2 + (nz - 1) + (plane - 1))

    width = REACH * block
    pieces = deg.shape[0]
    sends = [
        remote(basis_hbm.at[:, pl.ds((count - REACH) * block, width)], halo.at[0],
               halo_send.at[0], halo_recv.at[0], right),
        remote(basis_hbm.at[:, pl.ds(0, width)], halo.at[1],
               halo_send.at[1], halo_recv.at[1], left),
        remote(deg_hbm.at[pieces - 1], halo_deg.at[0], halo_send.at[2], halo_recv.at[2], right),
        remote(deg_hbm.at[0], halo_deg.at[1], halo_send.at[3], halo_recv.at[3], left),
    ]
    for copy in sends:
        copy.start()

    def spread(root, first_row):
        return jnp.concatenate(
            [root[first_row + h : first_row + h + 1, :] for h in range(block // 128)], axis=1)

    def scaled(raw, factor):
        return (raw.astype(F32) * factor).astype(BF16)

    per_block = block // 128
    deg_in.wait()
    for g in range(pieces):
        root = lax.rsqrt(deg[g].astype(F32))
        for j in range(REACH):
            iroot[g * REACH + j] = spread(root, j * per_block)
    basis_in.wait()
    for b in range(count):
        ext[b + REACH] = scaled(basis[:, b * block : (b + 1) * block], iroot[b])
    cols_in.wait()

    first = linear * count

    def picked(k, b, low, high):
        return ext[jnp.clip(cols[k, b] - first + REACH, low, high)]

    def split(b, acc):
        image = acc * iroot[b]
        hi = image.astype(BF16)
        rest = image - hi.astype(F32)
        mid = rest.astype(BF16)
        lo = (rest - mid.astype(F32)).astype(BF16)
        parts[b, :rank, :] = hi
        parts[b, rank:, :] = mid
        return hi, mid, lo

    def gram_of(splits):
        hi, mid, lo = (jnp.concatenate(p, axis=1) for p in zip(*splits))
        g1 = dot_nt(jnp.concatenate([hi, mid, lo], axis=0), hi)
        g2 = dot_nt(jnp.concatenate([hi, mid], axis=0), mid)
        g3 = dot_nt(hi, lo)
        small = g1[2 * rank :] + g2[rank:] + g3
        cross = g1[rank : 2 * rank] + g2[:rank]
        return g1[:rank] + (cross + small)

    for b in inner:
        aff_in(b).wait()
    splits = []
    for b in inner:
        acc = dot_nt(ext[b + REACH], aff[b, 0])
        for k in range(1, 3):
            acc += dot_nt(picked(k, b, REACH, count + REACH - 1), aff[b, k])
        splits.append(split(b, acc))
    gram = gram_of(splits)
    for b in outer:
        aff_in(b).wait()
    starts = [dot_nt(ext[b + REACH], aff[b, 0]) for b in outer]

    for copy in sends:
        copy.wait_recv()
    for side, base in ((0, 0), (1, count + REACH)):
        root = lax.rsqrt(halo_deg[side].astype(F32))
        for j in range(REACH):
            ext[base + j] = scaled(
                halo[side, :, j * block : (j + 1) * block], spread(root, j * per_block))

    splits = []
    for b, acc in zip(outer, starts):
        for k in range(1, 3):
            acc += dot_nt(picked(k, b, 0, count + 2 * REACH - 1), aff[b, k])
        splits.append(split(b, acc))
    gram += gram_of(splits)

    half = rank // 2
    packed = jnp.concatenate([gram[:half], gram[half:]], axis=1)
    per = half // plane
    for q in range(plane):
        gpack[q] = packed[q * per : (q + 1) * per]

    for i, (device, q) in enumerate(zip(plane_ids, plane_slots)):
        remote(gpack.at[q], rs_buf.at[i], rs_send, rs_recv, device).start()

    reorder_in.wait()
    ids = lax.broadcasted_iota(jnp.int32, (block, block), 0)
    for b in range(count):
        pick = jnp.where(ids == reorder[b : b + 1, :], 1.0, 0.0).astype(BF16)
        perm_out[b] = dot(parts[b], pick).astype(BF16)

    drain(rs_buf, rs_recv)
    z_src[...] = gpack[mine] + jnp.sum(rs_buf[...], axis=0)
    for i, device in enumerate(z_ids):
        remote(z_src, z_buf.at[i], z_send, z_recv, device).start()
    for copy in sends:
        copy.wait_send()
    drain(rs_buf, rs_send)

    drain(z_buf, z_recv)
    chunk = z_src[...] + jnp.sum(z_buf[...], axis=0)
    ag_src[...] = chunk
    ag_buf[mine] = chunk
    for device in plane_ids:
        remote(ag_src, ag_buf.at[mine], ag_send, ag_recv, device).start()
    drain(z_buf, z_send)
    drain(ag_buf.at[pl.ds(0, plane - 1)], ag_recv)
    for q in range(plane):
        gram_out[q * per : (q + 1) * per] = ag_buf[q]
    drain(ag_buf.at[pl.ds(0, plane - 1)], ag_send)


def back_kernel(scale, gram_ref, perm, out_hbm, out, out_sem):
    count, depth, block = perm.shape
    rank = depth // 2
    half = rank // 2
    tiles = rank // 8

    packed = gram_ref[...]
    low = pltpu.roll(packed, rank, 1)
    lane = lax.broadcasted_iota(jnp.int32, (8, 2 * rank), 1)
    sublane = lax.broadcasted_iota(jnp.int32, (8, 2 * rank), 0)
    state = []
    for t in range(tiles):
        source = low if t < tiles // 2 else packed
        r = (8 * t) % half
        eye = jnp.where(lane == sublane + 8 * t, 1.0, 0.0)
        state.append(jnp.where(lane < rank, eye, source[r : r + 8]))

    def row(v, j):
        return jnp.broadcast_to(v[j : j + 1, :], v.shape)

    rows = []
    for t in range(tiles):
        cols = []
        for j in range(8):
            k = rank + 8 * t + j
            cols.append([jnp.broadcast_to(state[v][:, k : k + 1], (8, 2 * rank)) for v in range(t, tiles)])
        pivots = None
        mults = []
        pivot_rows = []
        for j in range(8):
            pivot = row(cols[j][0], j)
            pivots = pivot if pivots is None else jnp.where(sublane == j, pivot, pivots)
            inv = 1.0 / pivot
            mult = [c * inv for c in cols[j]]
            mult[0] = jnp.where(sublane > j, mult[0], 0.0)
            for jj in range(j + 1, 8):
                top = row(cols[jj][0], j)
                cols[jj] = [c - m * top for c, m in zip(cols[jj], mult)]
            pivot_row = row(state[t], j)
            state[t] = state[t] - mult[0] * pivot_row
            mults.append(mult)
            pivot_rows.append(pivot_row)
        for v in range(t + 1, tiles):
            upd = mults[0][v - t] * pivot_rows[0]
            for j in range(1, 8):
                upd = upd + mults[j][v - t] * pivot_rows[j]
            state[v] = state[v] - upd
        rows.append(state[t] * (lax.rsqrt(pivots) * scale))

    inverse = jnp.concatenate(rows, axis=0)[:, :rank]
    hi = inverse.astype(BF16)
    mid = (inverse - hi.astype(F32)).astype(BF16)
    left = jnp.concatenate(
        [jnp.concatenate([hi, hi], axis=1), jnp.concatenate([mid, mid], axis=1)], axis=0)

    def out_copy(b):
        cols = pl.ds(b * block, block)
        return pltpu.make_async_copy(out.at[:, cols], out_hbm.at[:, cols], out_sem.at[b])

    for b in range(count):
        both = dot(left, perm[b])
        out[:, b * block : (b + 1) * block] = both[:rank] + both[rank:]
        out_copy(b).start()
    for b in range(count):
        out_copy(b).wait()


def body(ny, nz, ns, affinity, old_basis, degrees, column_blocks, reorder):
    count, _, block, _ = affinity.shape
    rows_here, rank = old_basis.shape
    plane = ny * ns
    per = rank // 2 // plane
    anywhere = pl.BlockSpec(memory_space=pl.ANY)
    vmem = pl.BlockSpec(memory_space=pltpu.VMEM)
    dma = pltpu.SemaphoreType.DMA
    width = REACH * block // 128
    gram, perm = pl.pallas_call(
        functools.partial(front_kernel, (nz, ny, ns, count, block)),
        name="front",
        out_shape=(
            pltpu.VMEM((rank // 2, 2 * rank), F32),
            pltpu.VMEM((count, 2 * rank, block), BF16),
        ),
        in_specs=[anywhere] * 5,
        out_specs=(vmem, vmem),
        scratch_shapes=[
            pltpu.SMEM(column_blocks.shape[::-1], jnp.int32),
            pltpu.VMEM(affinity.shape, BF16),
            pltpu.VMEM((rank, rows_here), BF16),
            pltpu.VMEM((count // REACH, width, 128), jnp.int32),
            pltpu.VMEM(reorder.shape, jnp.int32),
            pltpu.VMEM((2, rank, REACH * block), BF16),
            pltpu.VMEM((2, width, 128), jnp.int32),
            pltpu.VMEM((count + 2 * REACH, rank, block), BF16),
            pltpu.VMEM((count, 1, block), F32),
            pltpu.VMEM((count, 2 * rank, block), BF16),
            pltpu.VMEM((plane, per, 2 * rank), F32),
            pltpu.VMEM((plane - 1, per, 2 * rank), F32),
            pltpu.VMEM((per, 2 * rank), F32),
            pltpu.VMEM((nz - 1, per, 2 * rank), F32),
            pltpu.VMEM((per, 2 * rank), F32),
            pltpu.VMEM((plane, per, 2 * rank), F32),
            dma((4,)), dma((count,)), dma((4,)), dma((4,)),
            dma, dma, dma, dma, dma, dma,
        ],
        compiler_params=pltpu.CompilerParams(collective_id=0, has_side_effects=True),
    )(column_blocks.T, affinity, old_basis.T, degrees.reshape(-1, width, 128), reorder)
    items = rows_here * lax.axis_size("rows") * lax.axis_size("sub")
    out = pl.pallas_call(
        functools.partial(back_kernel, math.sqrt(items)),
        name="back",
        out_shape=jax.ShapeDtypeStruct((rank, rows_here), F32),
        in_specs=[vmem, vmem],
        out_specs=anywhere,
        scratch_shapes=[pltpu.VMEM((rank, rows_here), F32), dma((count,))],
    )(*(pltpu.with_memory_space_constraint(a, pltpu.VMEM) for a in (gram, perm)))
    return out.T


def solution(mesh):
    rows, ns = mesh.shape["rows"], mesh.shape["sub"]
    nz = 16 if rows % 16 == 0 else rows // 2
    both = P(("rows", "sub"))
    return jax.shard_map(
        functools.partial(body, rows // nz, nz, ns),
        mesh=mesh, in_specs=(both,) * 5, out_specs=both, check_vma=False,
    )
```

time: 48.1 us -> 41.6 us (0.86)
  Pallas kernels: 47.8 us -> 41.5 us
    pallas_call x1, Pallas kernels: 42.7 us -> 38.6 us  [body(): pl.pallas_call(functools.partial(front_kernel, (nz, ny, ns, count, block)...]
    pallas_call x1, Pallas kernels: 5.15 us -> 2.87 us  [body(): pl.pallas_call(functools.partial(back_kernel, math.sqrt(items)), name='ba...]
where the time goes in v2:
time: 41.6 us; the launch traced here: 41.5 us
  Pallas kernels  41.5 us (100%)
    pallas_call x1, Pallas kernels, body(): pl.pallas_call(functools.partial(front_kernel, (nz, ny, ns, count, block)...  38.6 us
    pallas_call x1, Pallas kernels, body(): pl.pallas_call(functools.partial(back_kernel, math.sqrt(items)), name='ba...  2.87 us

profile of v2, /device:TPU:1, one launch (start us, length us, event | category | flops | bytes accessed | tf_op | source)
XLA Modules:
  0.0 41.5 jit_solution(17000069277427846117)
XLA Ops:
  0.0 38.6 %front.1 = (f32[32,128]{1,0:T(8,128)S(1)}, bf16[8,128,256]{2,1,0:T(8,128)(2,1)S(1)}) custom-call(s32[3,8]{1,0:T(4,128)} %bitcast.6, bf16[8,3,256,256]{3,2,1,0:T(8,128)(2,1)} %aff_hbm.1, bf16[64,2048]{1,0:T(8,128)(2,1)} %bitcast.4, s32[4,4,128]{2,1,0:T(4,128)} %bitcast.5, s32[8,256]{1,0:T(8,128)} %reorder_hbm.1), custom_call_target="tpu_custom_call" | custom-call | tf_op jit(solution)/shard_map/front/pallas_call | solution.py:297
  38.7 2.9 %back.1 = f32[64,2048]{1,0:T(8,128)} custom-call(f32[32,128]{1,0:T(8,128)S(1)} %get-tuple-element.7.gram_ref, bf16[8,128,256]{2,1,0:T(8,128)(2,1)S(1)} %get-tuple-element.8.perm), custom_call_target="tpu_custom_call" | custom-call | tf_op jit(solution)/shard_map/back/pallas_call | solution.py:329

commit v3 on v2

--- a/solution.py
+++ b/solution.py
@@ -37,7 +37,7 @@
     gram_out, perm_out,
     cols, aff, basis, deg, reorder, halo, halo_deg, ext, iroot, parts,
     gpack, rs_buf, z_src, z_buf, ag_src, ag_buf,
-    in_sem, aff_sem, halo_send, halo_recv, rs_send, rs_recv, z_send, z_recv, ag_send, ag_recv,
+    in_sem, aff_sem, halo_send, halo_recv, rs_send, rs_recv, z_send, z_recv, ag_send, ag_recv, far_sem,
 ):
     nz, ny, ns, count, block = dims
     plane = ny * ns
@@ -60,6 +60,8 @@
     plane_slots = [ys[dy] * ns + subs[ds] for dy, ds in plane_offsets]
     z_offsets = sorted(range(1, nz), key=lambda d: -around(d, nz))
     z_ids = [(y * nz + wrap(z + d, nz), sub) for d in z_offsets]
+    near = nz // 4 if nz >= 8 else nz
+    greeted = [device for d, device in zip(z_offsets, z_ids) if around(d, nz) <= near]
 
     barrier = pltpu.get_barrier_semaphore()
 
@@ -91,13 +93,13 @@
     cols_in.start()
     for b in inner:
         aff_in(b).start()
-    for device in plane_ids + z_ids:
+    for device in plane_ids + greeted:
         signal(device)
     for b in outer:
         aff_in(b).start()
     reorder_in.start()
 
-    pl.semaphore_wait(barrier, 2 + (nz - 1) + (plane - 1))
+    pl.semaphore_wait(barrier, 2 + len(greeted) + len(plane_ids))
 
     width = REACH * block
     pieces = deg.shape[0]
@@ -111,6 +113,10 @@
     ]
     for copy in sends:
         copy.start()
+    relays = [near, nz - near] if near < nz else []
+    for d in relays:
+        pl.semaphore_signal(
+            far_sem, inc=1, device_id=(y * nz + wrap(z + d, nz), sub), device_id_type=MESH)
 
     def spread(root, first_row):
         return jnp.concatenate(
@@ -198,6 +204,8 @@
         perm_out[b] = dot(parts[b], pick).astype(BF16)
 
     drain(rs_buf, rs_recv)
+    if relays:
+        pl.semaphore_wait(far_sem, len(relays))
     z_src[...] = gpack[mine] + jnp.sum(rs_buf[...], axis=0)
     for i, device in enumerate(z_ids):
         remote(z_src, z_buf.at[i], z_send, z_recv, device).start()
@@ -321,7 +329,7 @@
             pltpu.VMEM((per, 2 * rank), F32),
             pltpu.VMEM((plane, per, 2 * rank), F32),
             dma((4,)), dma((count,)), dma((4,)), dma((4,)),
-            dma, dma, dma, dma, dma, dma,
+            dma, dma, dma, dma, dma, dma, pltpu.SemaphoreType.REGULAR,
         ],
         compiler_params=pltpu.CompilerParams(collective_id=0, has_side_effects=True),
     )(column_blocks.T, affinity, old_basis.T, degrees.reshape(-1, width, 128), reorder)
@@ -339,7 +347,7 @@
 
 def solution(mesh):
     rows, ns = mesh.shape["rows"], mesh.shape["sub"]
-    nz = 16 if rows % 16 == 0 else rows // 2
+    nz = min(16, rows)
     both = P(("rows", "sub"))
     return jax.shard_map(
         functools.partial(body, rows // nz, nz, ns),

time: 41.6 us -> 39.8 us (0.957)
  Pallas kernels: 41.5 us -> 39.7 us
    pallas_call x1, Pallas kernels: 38.6 us -> 36.8 us  [body(): pl.pallas_call(functools.partial(front_kernel, (nz, ny, ns, count, block)...]
where the time goes in v3:
time: 39.8 us; the launch traced here: 39.7 us
  Pallas kernels  39.7 us (100%)
    pallas_call x1, Pallas kernels, body(): pl.pallas_call(functools.partial(front_kernel, (nz, ny, ns, count, block)...  36.8 us
    pallas_call x1, Pallas kernels, body(): pl.pallas_call(functools.partial(back_kernel, math.sqrt(items)), name='ba...  2.87 us

profile of v3, /device:TPU:1, one launch (start us, length us, event | category | flops | bytes accessed | tf_op | source)
XLA Modules:
  0.0 39.7 jit_solution(10964553917645972601)
XLA Ops:
  0.0 36.8 %front.1 = (f32[32,128]{1,0:T(8,128)S(1)}, bf16[8,128,256]{2,1,0:T(8,128)(2,1)S(1)}) custom-call(s32[3,8]{1,0:T(4,128)} %bitcast.6, bf16[8,3,256,256]{3,2,1,0:T(8,128)(2,1)} %aff_hbm.1, bf16[64,2048]{1,0:T(8,128)(2,1)} %bitcast.4, s32[4,4,128]{2,1,0:T(4,128)} %bitcast.5, s32[8,256]{1,0:T(8,128)} %reorder_hbm.1), custom_call_target="tpu_custom_call" | custom-call | tf_op jit(solution)/shard_map/front/pallas_call | solution.py:305
  36.9 2.9 %back.1 = f32[64,2048]{1,0:T(8,128)} custom-call(f32[32,128]{1,0:T(8,128)S(1)} %get-tuple-element.7.gram_ref, bf16[8,128,256]{2,1,0:T(8,128)(2,1)S(1)} %get-tuple-element.8.perm), custom_call_target="tpu_custom_call" | custom-call | tf_op jit(solution)/shard_map/back/pallas_call | solution.py:337

commit v4 on v2

--- a/solution.py
+++ b/solution.py
@@ -10,6 +10,7 @@
 
 MESH = pl.DeviceIdType.MESH
 REACH = 2
+DEPTHS = (2, 2, 2, 2)
 NT = (((1,), (1,)), ((), ()))
 F32 = jnp.float32
 BF16 = jnp.bfloat16
@@ -29,6 +30,12 @@
 
 def around(offset, size):
     return min(offset, size - offset)
+
+
+def tree_sum(terms):
+    while len(terms) > 1:
+        terms = [sum(terms[i : i + 2][1:], terms[i]) for i in range(0, len(terms), 2)]
+    return terms[0]
 
 
 def front_kernel(
@@ -37,7 +44,7 @@
     gram_out, perm_out,
     cols, aff, basis, deg, reorder, halo, halo_deg, ext, iroot, parts,
     gpack, rs_buf, z_src, z_buf, ag_src, ag_buf,
-    in_sem, aff_sem, halo_send, halo_recv, rs_send, rs_recv, z_send, z_recv, ag_send, ag_recv,
+    in_sem, aff_sem, halo_send, halo_recv, rs_send, rs_recv, z_send, z_recv, ag_send, ag_recv, plane_sem, far_sem,
 ):
     nz, ny, ns, count, block = dims
     plane = ny * ns
@@ -60,6 +67,15 @@
     plane_slots = [ys[dy] * ns + subs[ds] for dy, ds in plane_offsets]
     z_offsets = sorted(range(1, nz), key=lambda d: -around(d, nz))
     z_ids = [(y * nz + wrap(z + d, nz), sub) for d in z_offsets]
+    y_line = [(ys[d] * nz + z, sub) for d in range(1, ny)]
+    x_line = [(row, subs[d]) for d in range(1, ns)]
+
+    def z_id(d):
+        return (y * nz + wrap(z + d, nz), sub)
+
+    near = max(1, nz // 8)
+    steps = [near, 2 * near]
+    z_line = [z_id(d) for d in range(1, nz) if around(d, nz) <= near]
 
     barrier = pltpu.get_barrier_semaphore()
 
@@ -91,26 +107,34 @@
     cols_in.start()
     for b in inner:
         aff_in(b).start()
-    for device in plane_ids + z_ids:
+    for device in x_line + y_line + z_line:
         signal(device)
     for b in outer:
         aff_in(b).start()
     reorder_in.start()
 
-    pl.semaphore_wait(barrier, 2 + (nz - 1) + (plane - 1))
+    pl.semaphore_wait(barrier, 2 + len(x_line) + len(y_line) + len(z_line))
 
     width = REACH * block
     pieces = deg.shape[0]
     sends = [
-        remote(basis_hbm.at[:, pl.ds((count - REACH) * block, width)], halo.at[0],
+        remote(basis.at[:, pl.ds((count - REACH) * block, width)], halo.at[0],
                halo_send.at[0], halo_recv.at[0], right),
-        remote(basis_hbm.at[:, pl.ds(0, width)], halo.at[1],
+        remote(basis.at[:, pl.ds(0, width)], halo.at[1],
                halo_send.at[1], halo_recv.at[1], left),
         remote(deg_hbm.at[pieces - 1], halo_deg.at[0], halo_send.at[2], halo_recv.at[2], right),
         remote(deg_hbm.at[0], halo_deg.at[1], halo_send.at[3], halo_recv.at[3], left),
     ]
+    basis_in.wait()
     for copy in sends:
         copy.start()
+
+    def tell(sem, devices):
+        for device in devices:
+            pl.semaphore_signal(sem, inc=1, device_id=device, device_id_type=MESH)
+
+    tell(plane_sem, y_line)
+    tell(far_sem.at[0], [z_id(steps[0]), z_id(nz - steps[0])])
 
     def spread(root, first_row):
         return jnp.concatenate(
@@ -125,7 +149,6 @@
         root = lax.rsqrt(deg[g].astype(F32))
         for j in range(REACH):
             iroot[g * REACH + j] = spread(root, j * per_block)
-    basis_in.wait()
     for b in range(count):
         ext[b + REACH] = scaled(basis[:, b * block : (b + 1) * block], iroot[b])
     cols_in.wait()
@@ -167,6 +190,8 @@
         aff_in(b).wait()
     starts = [dot_nt(ext[b + REACH], aff[b, 0]) for b in outer]
 
+    pl.semaphore_wait(far_sem.at[0], 2)
+    tell(far_sem.at[1], [z_id(steps[1]), z_id(nz - steps[1])])
     for copy in sends:
         copy.wait_recv()
     for side, base in ((0, 0), (1, count + REACH)):
@@ -188,6 +213,8 @@
     for q in range(plane):
         gpack[q] = packed[q * per : (q + 1) * per]
 
+    if y_line:
+        pl.semaphore_wait(plane_sem, len(y_line))
     for i, (device, q) in enumerate(zip(plane_ids, plane_slots)):
         remote(gpack.at[q], rs_buf.at[i], rs_send, rs_recv, device).start()
 
@@ -198,7 +225,8 @@
         perm_out[b] = dot(parts[b], pick).astype(BF16)
 
     drain(rs_buf, rs_recv)
-    z_src[...] = gpack[mine] + jnp.sum(rs_buf[...], axis=0)
+    pl.semaphore_wait(far_sem.at[1], 2)
+    z_src[...] = tree_sum([gpack[mine]] + [rs_buf[i] for i in range(plane - 1)])
     for i, device in enumerate(z_ids):
         remote(z_src, z_buf.at[i], z_send, z_recv, device).start()
     for copy in sends:
@@ -206,7 +234,7 @@
     drain(rs_buf, rs_send)
 
     drain(z_buf, z_recv)
-    chunk = z_src[...] + jnp.sum(z_buf[...], axis=0)
+    chunk = tree_sum([z_src[...]] + [z_buf[i] for i in range(nz - 1)])
     ag_src[...] = chunk
     ag_buf[mine] = chunk
     for device in plane_ids:
@@ -239,33 +267,39 @@
         return jnp.broadcast_to(v[j : j + 1, :], v.shape)
 
     rows = []
-    for t in range(tiles):
+    start = 0
+    for depth in DEPTHS:
+        span = range(start, tiles)
         cols = []
-        for j in range(8):
-            k = rank + 8 * t + j
-            cols.append([jnp.broadcast_to(state[v][:, k : k + 1], (8, 2 * rank)) for v in range(t, tiles)])
-        pivots = None
+        for j in range(8 * depth):
+            k = rank + 8 * start + j
+            cols.append({v: jnp.broadcast_to(state[v][:, k : k + 1], (8, 2 * rank))
+                         for v in span if v >= start + j // 8})
         mults = []
         pivot_rows = []
-        for j in range(8):
-            pivot = row(cols[j][0], j)
-            pivots = pivot if pivots is None else jnp.where(sublane == j, pivot, pivots)
+        pivots = [None] * depth
+        for j in range(8 * depth):
+            t, i = start + j // 8, j % 8
+            pivot = row(cols[j][t], i)
+            d = j // 8
+            pivots[d] = pivot if i == 0 else jnp.where(sublane == i, pivot, pivots[d])
             inv = 1.0 / pivot
-            mult = [c * inv for c in cols[j]]
-            mult[0] = jnp.where(sublane > j, mult[0], 0.0)
-            for jj in range(j + 1, 8):
-                top = row(cols[jj][0], j)
-                cols[jj] = [c - m * top for c, m in zip(cols[jj], mult)]
-            pivot_row = row(state[t], j)
-            state[t] = state[t] - mult[0] * pivot_row
+            mult = {v: c * inv for v, c in cols[j].items()}
+            for jj in range(j + 1, 8 * depth):
+                top = row(cols[j][start + jj // 8], jj % 8)
+                cols[jj] = {v: c - mult[v] * top for v, c in cols[jj].items()}
+            mult[t] = jnp.where(sublane > i, mult[t], 0.0)
+            pivot_row = row(state[t], i)
+            for v in range(t, start + depth):
+                state[v] = state[v] - mult[v] * pivot_row
             mults.append(mult)
             pivot_rows.append(pivot_row)
-        for v in range(t + 1, tiles):
-            upd = mults[0][v - t] * pivot_rows[0]
-            for j in range(1, 8):
-                upd = upd + mults[j][v - t] * pivot_rows[j]
-            state[v] = state[v] - upd
-        rows.append(state[t] * (lax.rsqrt(pivots) * scale))
+        for v in range(start + depth, tiles):
+            for mult, pivot_row in zip(mults, pivot_rows):
+                state[v] = state[v] - mult[v] * pivot_row
+        for d in range(depth):
+            rows.append(state[start + d] * (lax.rsqrt(pivots[d]) * scale))
+        start += depth
 
     inverse = jnp.concatenate(rows, axis=0)[:, :rank]
     hi = inverse.astype(BF16)
@@ -322,6 +356,7 @@
             pltpu.VMEM((plane, per, 2 * rank), F32),
             dma((4,)), dma((count,)), dma((4,)), dma((4,)),
             dma, dma, dma, dma, dma, dma,
+            pltpu.SemaphoreType.REGULAR, pltpu.SemaphoreType.REGULAR((2,)),
         ],
         compiler_params=pltpu.CompilerParams(collective_id=0, has_side_effects=True),
     )(column_blocks.T, affinity, old_basis.T, degrees.reshape(-1, width, 128), reorder)
@@ -339,7 +374,7 @@
 
 def solution(mesh):
     rows, ns = mesh.shape["rows"], mesh.shape["sub"]
-    nz = 16 if rows % 16 == 0 else rows // 2
+    nz = min(16, rows)
     both = P(("rows", "sub"))
     return jax.shard_map(
         functools.partial(body, rows // nz, nz, ns),

time: 41.6 us -> 38.3 us (0.921)
  Pallas kernels: 41.5 us -> 38.2 us
    pallas_call x1, Pallas kernels: 38.6 us -> 35.6 us  [body(): pl.pallas_call(functools.partial(front_kernel, (nz, ny, ns, count, block)...]
where the time goes in v4:
time: 38.3 us; the launch traced here: 38.2 us
  Pallas kernels  38.2 us (100%)
    pallas_call x1, Pallas kernels, body(): pl.pallas_call(functools.partial(front_kernel, (nz, ny, ns, count, block)...  35.6 us
    pallas_call x1, Pallas kernels, body(): pl.pallas_call(functools.partial(back_kernel, math.sqrt(items)), name='ba...  2.59 us

profile of v4, /device:TPU:1, one launch (start us, length us, event | category | flops | bytes accessed | tf_op | source)
XLA Modules:
  0.0 38.2 jit_solution(2562350560539436849)
XLA Ops:
  0.0 35.6 %front.1 = (f32[32,128]{1,0:T(8,128)S(1)}, bf16[8,128,256]{2,1,0:T(8,128)(2,1)S(1)}) custom-call(s32[3,8]{1,0:T(4,128)} %bitcast.6, bf16[8,3,256,256]{3,2,1,0:T(8,128)(2,1)} %aff_hbm.1, bf16[64,2048]{1,0:T(8,128)(2,1)} %bitcast.4, s32[4,4,128]{2,1,0:T(4,128)} %bitcast.5, s32[8,256]{1,0:T(8,128)} %reorder_hbm.1), custom_call_target="tpu_custom_call" | custom-call | tf_op jit(solution)/shard_map/front/pallas_call | solution.py:331
  35.6 2.6 %back.1 = f32[64,2048]{1,0:T(8,128)} custom-call(f32[32,128]{1,0:T(8,128)S(1)} %get-tuple-element.7.gram_ref, bf16[8,128,256]{2,1,0:T(8,128)(2,1)S(1)} %get-tuple-element.8.perm), custom_call_target="tpu_custom_call" | custom-call | tf_op jit(solution)/shard_map/back/pallas_call | solution.py:364

commit v5 on v4

--- a/solution.py
+++ b/solution.py
@@ -10,6 +10,7 @@
 
 MESH = pl.DeviceIdType.MESH
 REACH = 2
+NY = 4
 DEPTHS = (2, 2, 2, 2)
 NT = (((1,), (1,)), ((), ()))
 F32 = jnp.float32
@@ -43,32 +44,35 @@
     cols_hbm, aff_hbm, basis_hbm, deg_hbm, reorder_hbm,
     gram_out, perm_out,
     cols, aff, basis, deg, reorder, halo, halo_deg, ext, iroot, parts,
-    gpack, rs_buf, z_src, z_buf, ag_src, ag_buf,
-    in_sem, aff_sem, halo_send, halo_recv, rs_send, rs_recv, z_send, z_recv, ag_send, ag_recv, plane_sem, far_sem,
+    gpack, core_buf, gsum, rs_buf, z_src, z_buf, ag_src, ag_buf,
+    in_sem, aff_sem, halo_send, halo_recv, core_send, core_recv, rs_send, rs_recv, z_send, z_recv, ag_send, ag_recv, plane_sem, far_sem,
 ):
     nz, ny, ns, count, block = dims
-    plane = ny * ns
-    total = plane * nz
+    nx = ns // 2
+    plane = ny * nx
+    total = ny * nz * ns
     rank = basis.shape[0]
     row, sub = lax.axis_index("rows"), lax.axis_index("sub")
     y, z = row // nz, row % nz
-    mine = y * ns + sub
+    x, core = sub // 2, sub % 2
+    mine = y * nx + x
     linear = row * ns + sub
 
     up, down = wrap(linear + 1, total), wrap(linear + total - 1, total)
     right = (up // ns, up % ns)
     left = (down // ns, down % ns)
     ys = [wrap(y + d, ny) for d in range(ny)]
-    subs = [wrap(sub + d, ns) for d in range(ns)]
+    xs = [wrap(x + d, nx) for d in range(nx)]
     plane_offsets = sorted(
-        ((dy, ds) for dy in range(ny) for ds in range(ns) if dy or ds),
-        key=lambda o: -(2 * around(o[0], ny) + around(o[1], ns)))
-    plane_ids = [(ys[dy] * nz + z, subs[ds]) for dy, ds in plane_offsets]
-    plane_slots = [ys[dy] * ns + subs[ds] for dy, ds in plane_offsets]
+        ((dy, dx) for dy in range(ny) for dx in range(nx) if dy or dx),
+        key=lambda o: -(around(o[0], ny) + around(o[1], nx)))
+    plane_ids = [(ys[dy] * nz + z, 2 * xs[dx] + core) for dy, dx in plane_offsets]
+    plane_slots = [ys[dy] * nx + xs[dx] for dy, dx in plane_offsets]
+    partner = (row, sub + 1 - 2 * core)
     z_offsets = sorted(range(1, nz), key=lambda d: -around(d, nz))
     z_ids = [(y * nz + wrap(z + d, nz), sub) for d in z_offsets]
     y_line = [(ys[d] * nz + z, sub) for d in range(1, ny)]
-    x_line = [(row, subs[d]) for d in range(1, ns)]
+    x_line = [(row, 2 * xs[d] + core) for d in range(1, nx)]
 
     def z_id(d):
         return (y * nz + wrap(z + d, nz), sub)
@@ -107,13 +111,13 @@
     cols_in.start()
     for b in inner:
         aff_in(b).start()
-    for device in x_line + y_line + z_line:
+    for device in [partner] + x_line + y_line + z_line:
         signal(device)
     for b in outer:
         aff_in(b).start()
     reorder_in.start()
 
-    pl.semaphore_wait(barrier, 2 + len(x_line) + len(y_line) + len(z_line))
+    pl.semaphore_wait(barrier, 3 + len(x_line) + len(y_line) + len(z_line))
 
     width = REACH * block
     pieces = deg.shape[0]
@@ -212,11 +216,15 @@
     per = half // plane
     for q in range(plane):
         gpack[q] = packed[q * per : (q + 1) * per]
+    swap = remote(gpack, core_buf, core_send, core_recv, partner)
+    swap.start()
+    swap.wait_recv()
+    gsum[...] = gpack[...] + core_buf[...]
 
     if y_line:
         pl.semaphore_wait(plane_sem, len(y_line))
     for i, (device, q) in enumerate(zip(plane_ids, plane_slots)):
-        remote(gpack.at[q], rs_buf.at[i], rs_send, rs_recv, device).start()
+        remote(gsum.at[q], rs_buf.at[i], rs_send, rs_recv, device).start()
 
     reorder_in.wait()
     ids = lax.broadcasted_iota(jnp.int32, (block, block), 0)
@@ -226,11 +234,12 @@
 
     drain(rs_buf, rs_recv)
     pl.semaphore_wait(far_sem.at[1], 2)
-    z_src[...] = tree_sum([gpack[mine]] + [rs_buf[i] for i in range(plane - 1)])
+    z_src[...] = tree_sum([gsum[mine]] + [rs_buf[i] for i in range(plane - 1)])
     for i, device in enumerate(z_ids):
         remote(z_src, z_buf.at[i], z_send, z_recv, device).start()
     for copy in sends:
         copy.wait_send()
+    swap.wait_send()
     drain(rs_buf, rs_send)
 
     drain(z_buf, z_recv)
@@ -322,7 +331,7 @@
 def body(ny, nz, ns, affinity, old_basis, degrees, column_blocks, reorder):
     count, _, block, _ = affinity.shape
     rows_here, rank = old_basis.shape
-    plane = ny * ns
+    plane = ny * (ns // 2)
     per = rank // 2 // plane
     anywhere = pl.BlockSpec(memory_space=pl.ANY)
     vmem = pl.BlockSpec(memory_space=pltpu.VMEM)
@@ -349,13 +358,15 @@
             pltpu.VMEM((count, 1, block), F32),
             pltpu.VMEM((count, 2 * rank, block), BF16),
             pltpu.VMEM((plane, per, 2 * rank), F32),
+            pltpu.VMEM((plane, per, 2 * rank), F32),
+            pltpu.VMEM((plane, per, 2 * rank), F32),
             pltpu.VMEM((plane - 1, per, 2 * rank), F32),
             pltpu.VMEM((per, 2 * rank), F32),
             pltpu.VMEM((nz - 1, per, 2 * rank), F32),
             pltpu.VMEM((per, 2 * rank), F32),
             pltpu.VMEM((plane, per, 2 * rank), F32),
             dma((4,)), dma((count,)), dma((4,)), dma((4,)),
-            dma, dma, dma, dma, dma, dma,
+            dma, dma, dma, dma, dma, dma, dma, dma,
             pltpu.SemaphoreType.REGULAR, pltpu.SemaphoreType.REGULAR((2,)),
         ],
         compiler_params=pltpu.CompilerParams(collective_id=0, has_side_effects=True),
@@ -374,7 +385,7 @@
 
 def solution(mesh):
     rows, ns = mesh.shape["rows"], mesh.shape["sub"]
-    nz = min(16, rows)
+    nz = rows // NY
     both = P(("rows", "sub"))
     return jax.shard_map(
         functools.partial(body, rows // nz, nz, ns),

time: 38.3 us -> 37.1 us (0.969)
  Pallas kernels: 38.2 us -> 36.9 us
    pallas_call x1, Pallas kernels: 35.6 us -> 34.4 us  [body(): pl.pallas_call(functools.partial(front_kernel, (nz, ny, ns, count, block)...]
where the time goes in v5:
time: 37.1 us; the launch traced here: 37 us
  Pallas kernels  36.9 us (99%)
    pallas_call x1, Pallas kernels, body(): pl.pallas_call(functools.partial(front_kernel, (nz, ny, ns, count, block)...  34.4 us
    pallas_call x1, Pallas kernels, body(): pl.pallas_call(functools.partial(back_kernel, math.sqrt(items)), name='ba...  2.59 us

profile of v5, /device:TPU:1, one launch (start us, length us, event | category | flops | bytes accessed | tf_op | source)
XLA Modules:
  0.0 37.0 jit_solution(5819493331736101423)
XLA Ops:
  0.0 34.4 %front.1 = (f32[32,128]{1,0:T(8,128)S(1)}, bf16[8,128,256]{2,1,0:T(8,128)(2,1)S(1)}) custom-call(s32[3,8]{1,0:T(4,128)} %bitcast.6, bf16[8,3,256,256]{3,2,1,0:T(8,128)(2,1)} %aff_hbm.1, bf16[64,2048]{1,0:T(8,128)(2,1)} %bitcast.4, s32[4,4,128]{2,1,0:T(4,128)} %bitcast.5, s32[8,256]{1,0:T(8,128)} %reorder_hbm.1), custom_call_target="tpu_custom_call" | custom-call | tf_op jit(solution)/shard_map/front/pallas_call | solution.py:340
  34.4 2.6 %back.1 = f32[64,2048]{1,0:T(8,128)} custom-call(f32[32,128]{1,0:T(8,128)S(1)} %get-tuple-element.7.gram_ref, bf16[8,128,256]{2,1,0:T(8,128)(2,1)S(1)} %get-tuple-element.8.perm), custom_call_target="tpu_custom_call" | custom-call | tf_op jit(solution)/shard_map/back/pallas_call | solution.py:375

commit v6 on v5

--- a/solution.py
+++ b/solution.py
@@ -44,8 +44,8 @@
     cols_hbm, aff_hbm, basis_hbm, deg_hbm, reorder_hbm,
     gram_out, perm_out,
     cols, aff, basis, deg, reorder, halo, halo_deg, ext, iroot, parts,
-    gpack, core_buf, gsum, rs_buf, z_src, z_buf, ag_src, ag_buf,
-    in_sem, aff_sem, halo_send, halo_recv, core_send, core_recv, rs_send, rs_recv, z_send, z_recv, ag_send, ag_recv, plane_sem, far_sem,
+    gpack, rs_buf, z_src, z_buf, ag_src, ag_buf,
+    in_sem, aff_sem, halo_send, halo_recv, rs_send, rs_recv, z_send, z_recv, ag_send, ag_recv, plane_sem, far_sem,
 ):
     nz, ny, ns, count, block = dims
     nx = ns // 2
@@ -67,12 +67,15 @@
         ((dy, dx) for dy in range(ny) for dx in range(nx) if dy or dx),
         key=lambda o: -(around(o[0], ny) + around(o[1], nx)))
     plane_ids = [(ys[dy] * nz + z, 2 * xs[dx] + core) for dy, dx in plane_offsets]
-    plane_slots = [ys[dy] * nx + xs[dx] for dy, dx in plane_offsets]
-    partner = (row, sub + 1 - 2 * core)
+    rs_targets = [
+        ((ys[dy] * nz + z, 2 * xs[dx] + c), ys[dy] * nx + xs[dx])
+        for dy, dx in plane_offsets for c in (core, 1 - core)]
+    partner = (row, 2 * x + 1 - core)
+    rs_targets.append((partner, mine))
     z_offsets = sorted(range(1, nz), key=lambda d: -around(d, nz))
     z_ids = [(y * nz + wrap(z + d, nz), sub) for d in z_offsets]
     y_line = [(ys[d] * nz + z, sub) for d in range(1, ny)]
-    x_line = [(row, 2 * xs[d] + core) for d in range(1, nx)]
+    x_line = [partner] + [(row, 2 * xs[d] + c) for d in range(1, nx) for c in (core, 1 - core)]
 
     def z_id(d):
         return (y * nz + wrap(z + d, nz), sub)
@@ -111,13 +114,13 @@
     cols_in.start()
     for b in inner:
         aff_in(b).start()
-    for device in [partner] + x_line + y_line + z_line:
+    for device in x_line + y_line + z_line:
         signal(device)
     for b in outer:
         aff_in(b).start()
     reorder_in.start()
 
-    pl.semaphore_wait(barrier, 3 + len(x_line) + len(y_line) + len(z_line))
+    pl.semaphore_wait(barrier, 2 + len(x_line) + len(y_line) + len(z_line))
 
     width = REACH * block
     pieces = deg.shape[0]
@@ -159,8 +162,14 @@
 
     first = linear * count
 
-    def picked(k, b, low, high):
-        return ext[jnp.clip(cols[k, b] - first + REACH, low, high)]
+    def place(k, b):
+        return cols[k, b] - first + REACH
+
+    def fetch(slot, low, high):
+        return ext[jnp.clip(slot, low, high)]
+
+    here = (REACH, count + REACH - 1)
+    anyone = (0, count + 2 * REACH - 1)
 
     def split(b, acc):
         image = acc * iroot[b]
@@ -187,12 +196,22 @@
     for b in inner:
         acc = dot_nt(ext[b + REACH], aff[b, 0])
         for k in range(1, 3):
-            acc += dot_nt(picked(k, b, REACH, count + REACH - 1), aff[b, k])
+            acc += dot_nt(fetch(place(k, b), *here), aff[b, k])
         splits.append(split(b, acc))
     gram = gram_of(splits)
     for b in outer:
         aff_in(b).wait()
-    starts = [dot_nt(ext[b + REACH], aff[b, 0]) for b in outer]
+    starts, pending = [], []
+    for b in outer:
+        acc = dot_nt(ext[b + REACH], aff[b, 0])
+        one, two = place(1, b), place(2, b)
+        if b in (REACH - 1, count - REACH):
+            away = (one < here[0]) | (one > here[1])
+            acc += dot_nt(fetch(jnp.where(away, two, one), *here), aff[b, jnp.where(away, 2, 1)])
+            pending.append([(jnp.where(away, one, two), jnp.where(away, 1, 2))])
+        else:
+            pending.append([(one, 1), (two, 2)])
+        starts.append(acc)
 
     pl.semaphore_wait(far_sem.at[0], 2)
     tell(far_sem.at[1], [z_id(steps[1]), z_id(nz - steps[1])])
@@ -205,9 +224,9 @@
                 halo[side, :, j * block : (j + 1) * block], spread(root, j * per_block))
 
     splits = []
-    for b, acc in zip(outer, starts):
-        for k in range(1, 3):
-            acc += dot_nt(picked(k, b, 0, count + 2 * REACH - 1), aff[b, k])
+    for b, acc, terms in zip(outer, starts, pending):
+        for slot, k in terms:
+            acc += dot_nt(fetch(slot, *anyone), aff[b, k])
         splits.append(split(b, acc))
     gram += gram_of(splits)
 
@@ -216,15 +235,11 @@
     per = half // plane
     for q in range(plane):
         gpack[q] = packed[q * per : (q + 1) * per]
-    swap = remote(gpack, core_buf, core_send, core_recv, partner)
-    swap.start()
-    swap.wait_recv()
-    gsum[...] = gpack[...] + core_buf[...]
 
     if y_line:
         pl.semaphore_wait(plane_sem, len(y_line))
-    for i, (device, q) in enumerate(zip(plane_ids, plane_slots)):
-        remote(gsum.at[q], rs_buf.at[i], rs_send, rs_recv, device).start()
+    for i, (device, q) in enumerate(rs_targets):
+        remote(gpack.at[q], rs_buf.at[i], rs_send, rs_recv, device).start()
 
     reorder_in.wait()
     ids = lax.broadcasted_iota(jnp.int32, (block, block), 0)
@@ -234,12 +249,11 @@
 
     drain(rs_buf, rs_recv)
     pl.semaphore_wait(far_sem.at[1], 2)
-    z_src[...] = tree_sum([gsum[mine]] + [rs_buf[i] for i in range(plane - 1)])
+    z_src[...] = tree_sum([gpack[mine]] + [rs_buf[i] for i in range(len(rs_targets))])
     for i, device in enumerate(z_ids):
         remote(z_src, z_buf.at[i], z_send, z_recv, device).start()
     for copy in sends:
         copy.wait_send()
-    swap.wait_send()
     drain(rs_buf, rs_send)
 
     drain(z_buf, z_recv)
@@ -249,10 +263,10 @@
     for device in plane_ids:
         remote(ag_src, ag_buf.at[mine], ag_send, ag_recv, device).start()
     drain(z_buf, z_send)
+    drain(ag_buf.at[pl.ds(0, plane - 1)], ag_send)
     drain(ag_buf.at[pl.ds(0, plane - 1)], ag_recv)
     for q in range(plane):
         gram_out[q * per : (q + 1) * per] = ag_buf[q]
-    drain(ag_buf.at[pl.ds(0, plane - 1)], ag_send)
 
 
 def back_kernel(scale, gram_ref, perm, out_hbm, out, out_sem):
@@ -358,15 +372,13 @@
             pltpu.VMEM((count, 1, block), F32),
             pltpu.VMEM((count, 2 * rank, block), BF16),
             pltpu.VMEM((plane, per, 2 * rank), F32),
-            pltpu.VMEM((plane, per, 2 * rank), F32),
-            pltpu.VMEM((plane, per, 2 * rank), F32),
-            pltpu.VMEM((plane - 1, per, 2 * rank), F32),
+            pltpu.VMEM((2 * plane - 1, per, 2 * rank), F32),
             pltpu.VMEM((per, 2 * rank), F32),
             pltpu.VMEM((nz - 1, per, 2 * rank), F32),
             pltpu.VMEM((per, 2 * rank), F32),
             pltpu.VMEM((plane, per, 2 * rank), F32),
             dma((4,)), dma((count,)), dma((4,)), dma((4,)),
-            dma, dma, dma, dma, dma, dma, dma, dma,
+            dma, dma, dma, dma, dma, dma,
             pltpu.SemaphoreType.REGULAR, pltpu.SemaphoreType.REGULAR((2,)),
         ],
         compiler_params=pltpu.CompilerParams(collective_id=0, has_side_effects=True),

time: 37.1 us -> 36.7 us (0.989)
    pallas_call x1, Pallas kernels: 34.4 us -> 34 us  [body(): pl.pallas_call(functools.partial(front_kernel, (nz, ny, ns, count, block)...]
where the time goes in v6:
time: 36.7 us; the launch traced here: 36.6 us
  Pallas kernels  36.6 us (100%)
    pallas_call x1, Pallas kernels, body(): pl.pallas_call(functools.partial(front_kernel, (nz, ny, ns, count, block)...  34 us
    pallas_call x1, Pallas kernels, body(): pl.pallas_call(functools.partial(back_kernel, math.sqrt(items)), name='ba...  2.59 us

profile of v6, /device:TPU:1, one launch (start us, length us, event | category | flops | bytes accessed | tf_op | source)
XLA Modules:
  0.0 36.6 jit_solution(497008728012178801)
XLA Ops:
  0.0 34.0 %front.1 = (f32[32,128]{1,0:T(8,128)S(1)}, bf16[8,128,256]{2,1,0:T(8,128)(2,1)S(1)}) custom-call(s32[3,8]{1,0:T(4,128)} %bitcast.6, bf16[8,3,256,256]{3,2,1,0:T(8,128)(2,1)} %aff_hbm.1, bf16[64,2048]{1,0:T(8,128)(2,1)} %bitcast.4, s32[4,4,128]{2,1,0:T(4,128)} %bitcast.5, s32[8,256]{1,0:T(8,128)} %reorder_hbm.1), custom_call_target="tpu_custom_call" | custom-call | tf_op jit(solution)/shard_map/front/pallas_call | solution.py:354
  34.0 2.6 %back.1 = f32[64,2048]{1,0:T(8,128)} custom-call(f32[32,128]{1,0:T(8,128)S(1)} %get-tuple-element.7.gram_ref, bf16[8,128,256]{2,1,0:T(8,128)(2,1)S(1)} %get-tuple-element.8.perm), custom_call_target="tpu_custom_call" | custom-call | tf_op jit(solution)/shard_map/back/pallas_call | solution.py:387
